TPU v7x, 128 devices: a whole 4x4x4 slice. The times are simulated.
128 devices in a mesh: row: 8 (over x, core), col: 16 (over y, z).
Axes of the slice: x: 4, y: 4, z: 4, core: 2. Of those that a mesh axis runs over, the one named last changes fastest.
Arguments:
- density_factor: bfloat16 [524288, 256], P(('row', 'col'))
- onsite: float32 [524288], P(('row', 'col')), may hold values from -4 to 4
- neighbour_ids: int32 [1024, 8], P(('row', 'col')), may hold values from 0 to 1023, as said below
- neighbour_count: int32 [1024], P(('row', 'col')), may hold values from 1 to 8, as said below
- coupling_type: int32 [1024, 8], P(('row', 'col')), may hold values from 0 to 3
- coupling_blocks: bfloat16 [4, 512, 512], replicated, may hold values from -0.25 to 0.25
- bath_pattern: int32 [1024], P(('row', 'col')), may hold values from 0 to 3
- bath_blocks: bfloat16 [4, 512, 512], replicated, may hold values from -0.25 to 0.25
Outputs:
- new_factor: bfloat16 [524288, 256], P(('row', 'col'))
Inputs may be any that keep to these rules, and one draw needn't show every extreme that they name: `neighbour_ids`: every neighbour of block b lies among the 128 blocks that share b's index of row, at most half of 128 blocks from b when that group is taken as a loop, and is never b itself; some block has a neighbour exactly half of 128 blocks away. Only the first neighbour_count[b] slots of block b's lists are used; some block uses all 8.
All inputs are finite; a program needn't handle non-finite values.
Results may differ from a plain program's by a relative error of at most 0.0056.
Values may be sent and summed in bfloat16 or wider, within the bound.
A program may use at most 192 MiB of HBM per device.

v0:
```python
import jax
import jax.numpy as jnp
from jax import lax
from jax.sharding import PartitionSpec as P

SWEEPS = 2
time_step = 0.25


def orthonormal_steps(gram, rank_cols):
    basis = jnp.eye(2 * rank_cols, rank_cols, dtype=jnp.float32)
    for sweep in range(SWEEPS):
        image = jnp.dot(gram, basis, precision=lax.Precision.HIGHEST)
        inner = jnp.dot(image.T, image, precision=lax.Precision.HIGHEST)
        factor = jnp.linalg.cholesky(inner)
        basis = lax.linalg.triangular_solve(
            factor, image, left_side=False, lower=True, transpose_a=True
        )
    return basis


def shards(
    density_factor,
    onsite,
    neighbour_ids,
    neighbour_count,
    coupling_type,
    coupling_blocks,
    bath_pattern,
    bath_blocks,
):
    blocks, slots = neighbour_ids.shape
    kinds = coupling_blocks.shape[0]
    block_rows = coupling_blocks.shape[1]
    rank_cols = density_factor.shape[1]
    col_count = lax.axis_size("col")
    group_blocks = col_count * blocks
    row_place = lax.axis_index("row")
    in_group = neighbour_ids - row_place * group_blocks
    slot_live = jnp.arange(slots, dtype=jnp.int32)[None, :] < neighbour_count[:, None]
    kind_match = (
        coupling_type[:, :, None] == jnp.arange(kinds, dtype=jnp.int32)[None, None, :]
    ) & slot_live[:, :, None]
    kind_float = kind_match.astype(jnp.float32)
    gathered = lax.all_gather(density_factor, "col", axis=0, tiled=True)
    hits = (
        in_group[:, :, None] == jnp.arange(group_blocks, dtype=jnp.int32)[None, None, :]
    ).astype(jnp.float32)
    mixing = jnp.einsum("bkt,bkn->btn", kind_float, hits).astype(jnp.bfloat16)
    flat_blocks = gathered.reshape(group_blocks, block_rows * rank_cols)
    summed = jnp.einsum("btn,nm->btm", mixing, flat_blocks, preferred_element_type=jnp.float32)
    summed = summed.reshape(blocks, kinds, block_rows, rank_cols).astype(jnp.bfloat16)
    coupled = jnp.einsum(
        "tij,btjr->bir", coupling_blocks, summed, preferred_element_type=jnp.float32
    )
    own_rows = density_factor.reshape(blocks, block_rows, rank_cols)
    bath_pick = bath_blocks[bath_pattern]
    bathed = jnp.einsum(
        "bij,bjr->bir", bath_pick, own_rows, preferred_element_type=jnp.float32
    ).astype(jnp.bfloat16)
    factor_wide = own_rows.astype(jnp.float32)
    energy = onsite.reshape(blocks, block_rows, 1)
    moved = (factor_wide - time_step * (energy * factor_wide + coupled)).astype(jnp.bfloat16)
    stacked = jnp.concatenate([moved, bathed], axis=2).reshape(blocks * block_rows, 2 * rank_cols)
    local_gram = lax.dot_general(
        stacked, stacked, (((0,), (0,)), ((), ())), preferred_element_type=jnp.float32
    )
    gram_sum = lax.psum(local_gram, ("row", "col"))
    rotation = orthonormal_steps(gram_sum, rank_cols).astype(jnp.bfloat16)
    return jnp.dot(stacked, rotation, preferred_element_type=jnp.float32).astype(jnp.bfloat16)


def solution(mesh):
    placed = (
        P(("row", "col"), None),
        P(("row", "col")),
        P(("row", "col"), None),
        P(("row", "col")),
        P(("row", "col"), None),
        P(),
        P(("row", "col")),
        P(),
    )
    return jax.shard_map(
        shards, mesh=mesh, in_specs=placed, out_specs=P(("row", "col"), None), check_vma=False
    )
```

profile of v0, /device:TPU:1, one launch (start us, length us, event | category | flops | bytes accessed | tf_op | source)
XLA Modules:
  0.0 618.0 jit_solution(14788270948122039171)
XLA Ops:
  8.0 3.9 copy.12
  12.0 2.9 gather_fusion
  14.9 4.2 convolution_convert_fusion.1
  19.1 190.8 %all-gather.2.cloned.1.call-done = bf16[65536,256]{1,0:T(8,128)(2,1)} async-done(((bf16[4096,256]{1,0:T(8,128)(2,1)}), bf16[65536,256]{1,0:T(8,128)(2,1)}) %all-gather.2.cloned.1.call-update) | async-done | bytes 33554448 | tf_op jit(solution)/shard_map/all_gather | solution.py:45
  210.0 33.2 %reshape.54 = bf16[128,131072]{1,0:T(8,128)(2,1)} reshape(bf16[65536,256]{1,0:T(8,128)(2,1)} %all-gather.2.cloned.1.call-done) | data formatting | bytes 67108864 | tf_op jit(solution)/shard_map/reshape | solution.py:50
  243.2 23.1 %copy.24 = bf16[16,8,512,256]{3,2,1,0:T(8,128)(2,1)} copy(bf16[16,8,512,256]{3,1,2,0:T(8,128)(2,1)} %bitcast.98) | data formatting | bytes 67108864
  266.2 36.0 %fusion = bf16[8,4,512,256]{3,1,2,0:T(4,128)(2,1)} fusion(bf16[512,256,128,1]{1,0,2,3:T(8,128)(2,1)} %bitcast.99, s32[8,8]{1,0:T(8,128)S(1)} %broadcast_subtract_fusion, s32[8,8]{1,0:T(8,128)S(1)} %copy-done.5, pred[8,8]{1,0:T(8,128)(4,1)S(1)} %iota_compare_fusion.9), kind=kOutput, calls=%fused_computation.5 | convolution fusion | flops 1073820160 | bytes 41943616 | tf_op jit(solution)/shard_map/btn,nm->btm/dot_general | solution.py:51
  302.3 13.8 %copy.20 = bf16[8,4,512,256]{2,3,1,0:T(8,128)(2,1)} copy(bf16[8,4,512,256]{3,1,2,0:T(4,128)(2,1)} %fusion) | data formatting | bytes 16777216 | tf_op jit(solution)/shard_map/btn,nm->btm/dot_general | solution.py:51
  316.1 9.6 %fusion.6 = bf16[8,512,256]{1,2,0:T(8,128)(2,1)S(1)} fusion(bf16[8,512,256]{1,2,0:T(8,128)(2,1)} %copy.12, bf16[8,4,512,256]{2,3,1,0:T(8,128)(2,1)} %copy.20, bf16[4,512,512]{2,1,0:T(8,128)(2,1)} %param.16, f32[8,512]{1,0:T(8,128)S(1)} %mul.19), kind=kOutput, calls=%fused_computation.14 | convolution fusion | flops 4301258752 | bytes 14696448 | tf_op jit(solution)/shard_map/tij,btjr->bir/dot_general | solution.py:53
  325.7 1.3 copy-done.3
  327.0 3.3 convolution_bitcast_fusion
  330.3 3.8 pad_maximum_fusion
  334.2 6.5 %copy.14 = bf16[8,512,512]{2,1,0:T(8,128)(2,1)} copy(bf16[8,512,512]{1,2,0:T(8,128)(2,1)} %pad_maximum_fusion) | data formatting | bytes 8388608 | tf_op jit(solution)/shard_map/concatenate | solution.py:64
  340.6 136.9 %all-reduce.3.cloned.1.call-done = f32[512,512]{1,0:T(8,128)} async-done(((f32[512,512]{1,0:T(8,128)}), f32[512,512]{1,0:T(8,128)}) %all-reduce.3.cloned.1.call-update) | async-done | bytes 1048592 | tf_op jit(solution)/shard_map/psum | solution.py:68
  477.5 1.9 fusion.15
  479.4 1.0 fusion.49
  480.7 11.7 %cholesky.130 = f32[128,128]{1,0:T(8,128)S(1)} custom-call(f32[128,128]{1,0:T(8,128)S(1)} %cholesky.194), custom_call_target="Cholesky" | custom-call | tf_op jit(solution)/shard_map/jit(cholesky)/cholesky | solution.py:15
  492.4 9.8 %custom-call.13 = f32[1,128,128]{1,2,0:T(8,128)S(1)} custom-call(f32[1,128,128]{2,1,0:T(8,128)S(1)} %get-tuple-element.50), custom_call_target="InvertDiagBlocksLowerTriangular" | custom-call | tf_op jit(solution)/shard_map/jit(cholesky)/cholesky | solution.py:15
  502.7 11.7 %cholesky.147 = f32[128,128]{1,0:T(8,128)S(1)} custom-call(f32[128,128]{1,0:T(8,128)S(1)} %convolution_subtract_fusion.3), custom_call_target="Cholesky" | custom-call | tf_op jit(solution)/shard_map/jit(cholesky)/cholesky | solution.py:15
  516.6 4.0 while.4
  517.2 1.4 bitcast_dynamic-update-slice_fusion.4
  519.2 1.4 bitcast_dynamic-update-slice_fusion.4
  520.6 20.1 %custom-call.14 = f32[2,128,128]{1,2,0:T(8,128)S(1)} custom-call(f32[2,128,128]{2,1,0:T(8,128)S(1)} %get-tuple-element.21), custom_call_target="InvertDiagBlocksLowerTriangular" | custom-call | tf_op jit(solution)/shard_map/triangular_solve/custom-call.0 | solution.py:16
  543.1 1.0 fusion.50
  544.3 11.7 %cholesky.164 = f32[128,128]{1,0:T(8,128)S(1)} custom-call(f32[128,128]{1,0:T(8,128)S(1)} %cholesky.197), custom_call_target="Cholesky" | custom-call | tf_op jit(solution)/shard_map/jit(cholesky)/cholesky | solution.py:15
  556.7 9.8 %custom-call.15 = f32[1,128,128]{1,2,0:T(8,128)S(1)} custom-call(f32[1,128,128]{2,1,0:T(8,128)S(1)} %get-tuple-element.46), custom_call_target="InvertDiagBlocksLowerTriangular" | custom-call | tf_op jit(solution)/shard_map/jit(cholesky)/cholesky | solution.py:15
  567.1 11.9 %cholesky.181 = f32[128,128]{1,0:T(8,128)S(1)} custom-call(f32[128,128]{1,0:T(8,128)S(1)} %convolution_subtract_fusion.2), custom_call_target="Cholesky" | custom-call | tf_op jit(solution)/shard_map/jit(cholesky)/cholesky | solution.py:15
  580.9 3.9 while.5
  581.5 1.4 bitcast_dynamic-update-slice_fusion.5
  583.5 1.4 bitcast_dynamic-update-slice_fusion.5
  584.9 19.7 %custom-call.16 = f32[2,128,128]{1,2,0:T(8,128)S(1)} custom-call(f32[2,128,128]{2,1,0:T(8,128)S(1)} %get-tuple-element.22), custom_call_target="InvertDiagBlocksLowerTriangular" | custom-call | tf_op jit(solution)/shard_map/triangular_solve/custom-call.0 | solution.py:16
  606.0 4.9 convolution_convert_fusion
  (64 shorter events, 11.4 us)
Async XLA Ops:
  6.5 5.4 copy-start
  6.5 5.4 copy-start.6
  6.5 203.4 %all-gather.2.cloned.1.call-start = ((), (), s32[]{:S(2)}) async-start(), calls=%async_computation | async-start | bytes 35651584 | tf_op jit(solution)/shard_map/all_gather | solution.py:45
  7.3 470.3 %all-reduce.3.cloned.1.call-start = ((), (), s32[]{:S(2)}) async-start(), calls=%async_computation.1 | async-start | bytes 2097152 | tf_op jit(solution)/shard_map/psum | solution.py:68
  12.0 2.9 copy-start.7
  12.0 3.0 copy-start.4
  243.2 23.1 %copy-start.5 = (s32[8,8]{1,0:T(8,128)S(1)}, s32[8,8]{1,0:T(8,128)}, u32[]{:S(2)}) copy-start(s32[8,8]{1,0:T(8,128)} %param.15) | copy-start | bytes 772
  325.6 1.3 copy-start.3
  477.5 64.6 %copy-start.2 = (f32[512,512]{1,0:T(8,128)S(1)}, f32[512,512]{1,0:T(8,128)}, u32[]{:S(2)}) copy-start(f32[512,512]{1,0:T(8,128)} %all-reduce.3.cloned.1.call-done) | copy-start | bytes 3145732
  606.0 5.0 copy-start.1
Sparse Core Ops, SparseCore 0:
  9.5 200.4 all-gather.1
  330.4 147.0 all-reduce.2
where the time goes:
time: 623 us; the launch traced here: 618 us
  waiting for transfers between devices  328 us (53%)
  other arithmetic  113 us (18%)
  local copies, waits for them, and re-layouts  93.6 us (15%)
  matrix products  66.8 us (11%)
  between operations  16.5 us (3%)
    all_gather x1, waiting for transfers between devices, shards(): gathered = lax.all_gather(density_factor, 'col', axis=0, tiled=True)  191 us
    psum x1, waiting for transfers between devices, shards(): gram_sum = lax.psum(local_gram, ('row', 'col'))  137 us
    another operation x13, other arithmetic, orthonormal_steps(): factor = jnp.linalg.cholesky(inner)  68.8 us
    another operation x5, other arithmetic, orthonormal_steps(): lax.linalg.triangular_solve(factor, image, left_side=False, lower=True, t...  39.8 us
    dot_general x1, matrix products, shards(): jnp.einsum('btn,nm->btm', mixing, flat_blocks, preferred_element_type=jnp...  36 us
    reshape x1, local copies, waits for them, and re-layouts, shards(): flat_blocks = gathered.reshape(group_blocks, block_rows * rank_cols)  33.2 us
    unnamed x17, local copies, waits for them, and re-layouts  24.4 us
    dot_general x1, local copies, waits for them, and re-layouts, shards(): jnp.einsum('btn,nm->btm', mixing, flat_blocks, preferred_element_type=jnp...  13.8 us
  transfers between devices with their start and end apart: 2, of which 2 were waited for; matrix products, arithmetic and copies ran while one was open for 4% of the time, Pallas kernels for 0%

commit v1 on v0

--- a/solution.py
+++ b/solution.py
@@ -65,7 +65,7 @@
     local_gram = lax.dot_general(
         stacked, stacked, (((0,), (0,)), ((), ())), preferred_element_type=jnp.float32
     )
-    gram_sum = lax.psum(local_gram, ("row", "col"))
+    gram_sum = jnp.sum(lax.all_gather(local_gram, ("row", "col")), axis=0)
     rotation = orthonormal_steps(gram_sum, rank_cols).astype(jnp.bfloat16)
     return jnp.dot(stacked, rotation, preferred_element_type=jnp.float32).astype(jnp.bfloat16)
 

time: 623 us -> 798 us (1.28)
  waiting for transfers between devices: 328 us -> 466 us
  other arithmetic: 113 us -> 153 us
    all_gather x0 -> x1, waiting for transfers between devices: none -> 273 us  [shards(): gram_sum = jnp.sum(lax.all_gather(local_gram, ('row', 'col')), axis=0)]
    psum x1 -> x0, waiting for transfers between devices: 137 us -> none  [shards(): gram_sum = lax.psum(local_gram, ('row', 'col'))]
    reduce_sum x0 -> x1, other arithmetic: none -> 40.8 us  [shards(): gram_sum = jnp.sum(lax.all_gather(local_gram, ('row', 'col')), axis=0)]
  transfers between devices with their start and end apart: 2 -> 2, of which waited for: 2 -> 2; matrix products, arithmetic and copies ran while one was open for 4% -> 3% of each run, Pallas kernels for 0% -> 0%
where the time goes in v1:
time: 798 us; the launch traced here: 794 us
  waiting for transfers between devices  466 us (58%)
  other arithmetic  153 us (19%)
  local copies, waits for them, and re-layouts  92.8 us (12%)
  matrix products  65.6 us (8%)
  between operations  16.5 us (2%)
    all_gather x1, waiting for transfers between devices, shards(): gram_sum = jnp.sum(lax.all_gather(local_gram, ('row', 'col')), axis=0)  273 us
    all_gather x1, waiting for transfers between devices, shards(): gathered = lax.all_gather(density_factor, 'col', axis=0, tiled=True)  192 us
    another operation x13, other arithmetic, orthonormal_steps(): factor = jnp.linalg.cholesky(inner)  68.7 us
    reduce_sum x1, other arithmetic, shards(): gram_sum = jnp.sum(lax.all_gather(local_gram, ('row', 'col')), axis=0)  40.8 us
    another operation x5, other arithmetic, orthonormal_steps(): lax.linalg.triangular_solve(factor, image, left_side=False, lower=True, t...  39.8 us
    dot_general x1, matrix products, shards(): jnp.einsum('btn,nm->btm', mixing, flat_blocks, preferred_element_type=jnp...  36 us
    reshape x1, local copies, waits for them, and re-layouts, shards(): flat_blocks = gathered.reshape(group_blocks, block_rows * rank_cols)  33.2 us
    unnamed x17, local copies, waits for them, and re-layouts  24.4 us
  transfers between devices with their start and end apart: 2, of which 2 were waited for; matrix products, arithmetic and copies ran while one was open for 3% of the time, Pallas kernels for 0%

profile of v1, /device:TPU:1, one launch (start us, length us, event | category | flops | bytes accessed | tf_op | source)
XLA Modules:
  0.0 793.9 jit_solution(13330452660732497303)
XLA Ops:
  7.3 3.9 copy.12
  11.3 2.9 gather_fusion
  14.3 4.2 convolution_convert_fusion.1
  18.4 191.5 %all-gather.4.cloned.1.call-done = bf16[65536,256]{1,0:T(8,128)(2,1)} async-done(((bf16[4096,256]{1,0:T(8,128)(2,1)}), bf16[65536,256]{1,0:T(8,128)(2,1)}) %all-gather.4.cloned.1.call-update) | async-done | bytes 33554448 | tf_op jit(solution)/shard_map/all_gather | solution.py:45
  210.0 33.2 %reshape.54 = bf16[128,131072]{1,0:T(8,128)(2,1)} reshape(bf16[65536,256]{1,0:T(8,128)(2,1)} %all-gather.4.cloned.1.call-done) | data formatting | bytes 67108864 | tf_op jit(solution)/shard_map/reshape | solution.py:50
  243.2 23.1 %copy.24 = bf16[16,8,512,256]{3,2,1,0:T(8,128)(2,1)} copy(bf16[16,8,512,256]{3,1,2,0:T(8,128)(2,1)} %bitcast.99) | data formatting | bytes 67108864
  266.2 36.0 %fusion = bf16[8,4,512,256]{3,1,2,0:T(4,128)(2,1)} fusion(bf16[512,256,128,1]{1,0,2,3:T(8,128)(2,1)} %bitcast.100, s32[8,8]{1,0:T(8,128)S(1)} %broadcast_subtract_fusion, s32[8,8]{1,0:T(8,128)S(1)} %copy-done.5, pred[8,8]{1,0:T(8,128)(4,1)S(1)} %iota_compare_fusion.9), kind=kOutput, calls=%fused_computation.5 | convolution fusion | flops 1073820160 | bytes 41943616 | tf_op jit(solution)/shard_map/btn,nm->btm/dot_general | solution.py:51
  302.3 13.8 %copy.20 = bf16[8,4,512,256]{2,3,1,0:T(8,128)(2,1)} copy(bf16[8,4,512,256]{3,1,2,0:T(4,128)(2,1)} %fusion) | data formatting | bytes 16777216 | tf_op jit(solution)/shard_map/btn,nm->btm/dot_general | solution.py:51
  316.1 9.6 %fusion.6 = bf16[8,512,256]{1,2,0:T(8,128)(2,1)S(1)} fusion(bf16[8,512,256]{1,2,0:T(8,128)(2,1)} %copy.12, bf16[8,4,512,256]{2,3,1,0:T(8,128)(2,1)} %copy.20, bf16[4,512,512]{2,1,0:T(8,128)(2,1)} %param.16, f32[8,512]{1,0:T(8,128)S(1)} %mul.19), kind=kOutput, calls=%fused_computation.14 | convolution fusion | flops 4301258752 | bytes 14696448 | tf_op jit(solution)/shard_map/tij,btjr->bir/dot_general | solution.py:53
  325.7 1.3 copy-done.2
  327.0 3.4 convolution_bitcast_fusion
  330.4 3.8 pad_maximum_fusion
  334.3 6.5 copy.14
  340.7 273.3 %all-gather.6.cloned.1.call-done = f32[65536,512]{1,0:T(8,128)} async-done(((f32[512,512]{1,0:T(8,128)}), f32[65536,512]{1,0:T(8,128)}) %all-gather.6.cloned.1.call-update) | async-done | bytes 134217744 | tf_op jit(solution)/shard_map/all_gather | solution.py:68
  614.1 40.8 %reduce_sum.9 = f32[512,512]{1,0:T(8,128)S(1)} reduce(f32[128,512,512]{2,1,0:T(8,128)} %bitcast.10, f32[]{:T(128)} %constant.70.clone.1), dimensions={0}, to_apply=%region_0.0 | reduce | flops 33292288 | bytes 135266304 | tf_op jit(solution)/shard_map/reduce_sum | solution.py:68
  655.4 1.0 fusion.49
  656.6 11.7 %cholesky.130 = f32[128,128]{1,0:T(8,128)S(1)} custom-call(f32[128,128]{1,0:T(8,128)S(1)} %cholesky.194), custom_call_target="Cholesky" | custom-call | tf_op jit(solution)/shard_map/jit(cholesky)/cholesky | solution.py:15
  668.4 9.8 %custom-call.13 = f32[1,128,128]{1,2,0:T(8,128)S(1)} custom-call(f32[1,128,128]{2,1,0:T(8,128)S(1)} %get-tuple-element.50), custom_call_target="InvertDiagBlocksLowerTriangular" | custom-call | tf_op jit(solution)/shard_map/jit(cholesky)/cholesky | solution.py:15
  678.7 11.7 %cholesky.147 = f32[128,128]{1,0:T(8,128)S(1)} custom-call(f32[128,128]{1,0:T(8,128)S(1)} %convolution_subtract_fusion.3), custom_call_target="Cholesky" | custom-call | tf_op jit(solution)/shard_map/jit(cholesky)/cholesky | solution.py:15
  692.5 4.0 while.4
  693.1 1.4 bitcast_dynamic-update-slice_fusion.4
  695.1 1.4 bitcast_dynamic-update-slice_fusion.4
  696.5 20.1 %custom-call.14 = f32[2,128,128]{1,2,0:T(8,128)S(1)} custom-call(f32[2,128,128]{2,1,0:T(8,128)S(1)} %get-tuple-element.21), custom_call_target="InvertDiagBlocksLowerTriangular" | custom-call | tf_op jit(solution)/shard_map/triangular_solve/custom-call.0 | solution.py:16
  719.0 1.0 fusion.50
  720.3 11.7 %cholesky.164 = f32[128,128]{1,0:T(8,128)S(1)} custom-call(f32[128,128]{1,0:T(8,128)S(1)} %cholesky.197), custom_call_target="Cholesky" | custom-call | tf_op jit(solution)/shard_map/jit(cholesky)/cholesky | solution.py:15
  732.0 9.8 %custom-call.15 = f32[1,128,128]{1,2,0:T(8,128)S(1)} custom-call(f32[1,128,128]{2,1,0:T(8,128)S(1)} %get-tuple-element.46), custom_call_target="InvertDiagBlocksLowerTriangular" | custom-call | tf_op jit(solution)/shard_map/jit(cholesky)/cholesky | solution.py:15
  742.3 11.8 %cholesky.181 = f32[128,128]{1,0:T(8,128)S(1)} custom-call(f32[128,128]{1,0:T(8,128)S(1)} %convolution_subtract_fusion.2), custom_call_target="Cholesky" | custom-call | tf_op jit(solution)/shard_map/jit(cholesky)/cholesky | solution.py:15
  756.8 4.0 while.5
  757.4 1.4 bitcast_dynamic-update-slice_fusion.5
  759.4 1.4 bitcast_dynamic-update-slice_fusion.5
  760.8 19.7 %custom-call.16 = f32[2,128,128]{1,2,0:T(8,128)S(1)} custom-call(f32[2,128,128]{2,1,0:T(8,128)S(1)} %get-tuple-element.22), custom_call_target="InvertDiagBlocksLowerTriangular" | custom-call | tf_op jit(solution)/shard_map/triangular_solve/custom-call.0 | solution.py:16
  781.9 4.9 convolution_convert_fusion
  (65 shorter events, 11.3 us)
Async XLA Ops:
  6.5 4.7 copy-start
  6.5 4.7 copy-start.3
  6.5 4.7 copy-start.6
  6.5 203.4 %all-gather.4.cloned.1.call-start = ((), (), s32[]{:S(2)}) async-start(), calls=%async_computation | async-start | bytes 35651584 | tf_op jit(solution)/shard_map/all_gather | solution.py:45
  7.3 606.8 %all-gather.6.cloned.1.call-start = ((), (), s32[]{:S(2)}) async-start(), calls=%async_computation.1 | async-start | bytes 135266304 | tf_op jit(solution)/shard_map/all_gather | solution.py:68
  11.3 2.9 copy-start.7
  11.3 3.0 copy-start.4
  243.2 23.1 %copy-start.5 = (s32[8,8]{1,0:T(8,128)S(1)}, s32[8,8]{1,0:T(8,128)}, u32[]{:S(2)}) copy-start(s32[8,8]{1,0:T(8,128)} %param.15) | copy-start | bytes 772
  325.6 1.3 copy-start.2
  781.9 5.0 copy-start.1
Sparse Core Ops, SparseCore 0:
  9.5 200.4 all-gather.3
  330.5 283.4 all-gather.5
